TPU v7x, 32 devices: a whole 2x2x4 slice. The times are simulated.
32 devices in a mesh: grp: 2 (over x), slab: 16 (over z, y, core).
Axes of the slice: x: 2, y: 2, z: 4, core: 2. Of those that a mesh axis runs over, the one named last changes fastest.
Arguments:
- image: float32 [2, 384, 192, 256], P(None, ('grp', 'slab')), parts along dimension 1, may hold values from -6 to 6
- adjoint_data: bfloat16 [2, 384, 192, 256], P(None, ('grp', 'slab')), parts along dimension 1, may hold values from -6 to 6
- coil_maps: bfloat16 [8, 2, 384, 192, 256], P(None, None, ('grp', 'slab')), parts along dimension 2, may hold values from -2.5 to 2.5
- masks: int32 [1, 384, 192], P(None, 'grp'), parts along dimension 1, may hold values 0 or 1
- sources: int32 [1, 1152, 2], P(None, ('grp', 'slab')), parts along dimension 1, may hold values from 0 to 575, as said below
- weights: bfloat16 [1, 1152, 8192], P(None, ('grp', 'slab')), parts along dimension 1, may hold values from -0.5 to 0.5
Outputs:
- updated: float32 [2, 384, 192, 256], P(None, ('grp', 'slab')), parts along dimension 1
There are 2 independent parts, one for each index of `grp`. A program takes and returns all parts, laid end to end along the dimension named above; each array names one. Nothing has to cross between parts.
Inputs may be any that keep to these rules, and one draw needn't show every extreme that they name: sources[s, t, j] is a block number (plane * 3 + y block); its plane lies within 24 planes of target block t's plane, and its y block within one of t's y block.
All inputs are finite; a program needn't handle non-finite values.
Results may differ from a plain program's by a relative error of at most 0.005.
Values may be sent and summed in bfloat16 or wider, within the bound.
No kernel may reach another device: no remote copies, remote signals or barrier semaphores. Data moves between devices by JAX's collectives and lax.ppermute only.
A program may use at most 256 MiB of HBM per device.

v0:
```python
import math
import jax
import jax.numpy as jnp
from jax import lax
from jax.sharding import PartitionSpec as P

NX = 192
NY = 192
NZ = 256
BLK = 64
REACH = 2


def shifted(shard, axis, by):
    count = lax.axis_size(axis)
    pairs = [(i, i + by) for i in range(count) if 0 <= i + by < count]
    return lax.ppermute(shard, axis, pairs)


def dft_table(length, direction):
    positions = jnp.arange(length, dtype=jnp.int32)
    product = positions[:, None] * positions[None, :] % length
    phases = product.astype(jnp.float32) * (2.0 * math.pi / length)
    factor = 1.0 / math.sqrt(length)
    cosine = jnp.cos(phases) * factor
    sine_part = jnp.sin(phases) * (direction * factor)
    upper_rows = jnp.stack([cosine, -sine_part], axis=1)
    lower_rows = jnp.stack([sine_part, cosine], axis=1)
    return jnp.stack([upper_rows, lower_rows], axis=0).astype(jnp.bfloat16)


def column_y(volume, matrix):
    return jnp.einsum("zcpxj,qkpj->zcqxk", volume, matrix, preferred_element_type=jnp.float32)


def column_x(volume, matrix):
    return jnp.einsum("zcpjy,qkpj->zcqky", volume, matrix, preferred_element_type=jnp.float32)


def expand_columns(sensitivity, warped):
    real_map = sensitivity[:, :, 0].astype(jnp.float32)
    imag_map = sensitivity[:, :, 1].astype(jnp.float32)
    real_warp = warped[:, 0][:, None]
    imag_warp = warped[:, 1][:, None]
    real_part = real_map * real_warp - imag_map * imag_warp
    imag_part = real_map * imag_warp + imag_map * real_warp
    return jnp.stack([real_part, imag_part], axis=2).astype(jnp.bfloat16)


def combine_columns(sensitivity, returned):
    real_map = sensitivity[:, :, 0].astype(jnp.float32)
    imag_map = sensitivity[:, :, 1].astype(jnp.float32)
    real_part = jnp.sum(real_map * returned[:, :, 0] + imag_map * returned[:, :, 1], axis=1)
    imag_part = jnp.sum(real_map * returned[:, :, 1] - imag_map * returned[:, :, 0], axis=1)
    return jnp.stack([real_part, imag_part], axis=1)


def per_device(image, adjoint_data, coil_maps, masks, sources, weights):
    slab_rank = lax.axis_index("slab")
    planes = image.shape[1]
    y_blocks = NY // BLK
    local_blocks = planes * y_blocks
    reach_slots = 2 * REACH + 1
    rounded = image.astype(jnp.bfloat16)
    forward_y = dft_table(NY, -1.0)
    inverse_y = dft_table(NY, 1.0)
    forward_x = dft_table(NX, -1.0)
    inverse_x = dft_table(NX, 1.0)
    nearby_list = []
    for offset in range(-REACH, REACH + 1):
        if offset == 0:
            nearby_list.append(rounded)
        else:
            nearby_list.append(shifted(rounded, "slab", -offset))
    nearby = jnp.stack(nearby_list, axis=1).reshape(2, reach_slots * local_blocks, BLK, NZ)
    maps_leading = jnp.transpose(coil_maps, (4, 0, 1, 2, 3))
    maps_columns = lax.all_to_all(maps_leading, "slab", split_axis=0, concat_axis=3, tiled=True)
    gradient = jnp.zeros((2, local_blocks, BLK, NZ), jnp.float32)
    link_ids = sources[0]
    matrices = weights[0].reshape(local_blocks, 2, BLK, BLK)
    positions = link_ids - (slab_rank - REACH) * local_blocks
    warped = jnp.zeros((2, local_blocks, BLK, NZ), jnp.float32)
    for member in range(2):
        picked = jnp.take(nearby, positions[:, member], axis=1)
        warped = warped + jnp.einsum(
            "tij,rtjz->rtiz", matrices[:, member], picked, preferred_element_type=jnp.float32
        )
    warped = warped.reshape(2, planes, NY, NZ)
    sampled = masks[0].astype(jnp.float32)
    warped_leading = jnp.transpose(warped, (3, 0, 1, 2))
    warped_columns = lax.all_to_all(warped_leading, "slab", split_axis=0, concat_axis=2, tiled=True)
    spectra = column_y(expand_columns(maps_columns, warped_columns), forward_y).astype(jnp.bfloat16)
    middle = (column_x(spectra, forward_x) * sampled[None, None, None, :, :]).astype(jnp.bfloat16)
    restored = column_x(middle, inverse_x).astype(jnp.bfloat16)
    combined_columns = combine_columns(maps_columns, column_y(restored, inverse_y)).astype(
        jnp.bfloat16
    )
    back_leading = lax.all_to_all(combined_columns, "slab", split_axis=2, concat_axis=0, tiled=True)
    grad_image = jnp.transpose(back_leading, (1, 2, 3, 0))
    grad_blocks = grad_image.reshape(2, local_blocks, BLK, NZ)
    spread = jnp.zeros((2, reach_slots * local_blocks, BLK, NZ), jnp.float32)
    for member in range(2):
        product = jnp.einsum(
            "tij,rtiz->rtjz", matrices[:, member], grad_blocks, preferred_element_type=jnp.float32
        )
        spread = spread.at[:, positions[:, member]].add(product)
    spread = spread.reshape(2, reach_slots, local_blocks, BLK, NZ)
    for offset in range(-REACH, REACH + 1):
        portion = spread[:, offset + REACH]
        if offset == 0:
            gradient = gradient + portion
        else:
            gradient = gradient + shifted(portion, "slab", offset)
    gradient = gradient.reshape(2, planes, NY, NZ)
    return image - 0.5 * (gradient - adjoint_data.astype(jnp.float32))


def solution(mesh):
    return jax.shard_map(
        per_device,
        mesh=mesh,
        in_specs=(
            P(None, ("grp", "slab"), None, None),
            P(None, ("grp", "slab"), None, None),
            P(None, None, ("grp", "slab"), None, None),
            P(None, "grp", None),
            P(None, ("grp", "slab"), None),
            P(None, ("grp", "slab"), None),
        ),
        out_specs=P(None, ("grp", "slab"), None, None),
        check_vma=False,
    )
```

profile of v0, /device:TPU:9, one launch (start us, length us, event | category | flops | bytes accessed | tf_op | source)
XLA Modules:
  0.0 1518.6 jit_solution(13383456892984787065)
XLA Ops:
  5.8 4.0 collective-permute-start.1
  17.7 113.8 %collective-permute-done = bf16[2,12,192,256]{3,2,1,0:T(8,128)(2,1)} collective-permute-done((bf16[2,12,192,256]{3,2,1,0:T(8,128)(2,1)S(1)}, bf16[2,12,192,256]{3,2,1,0:T(8,128)(2,1)}, u32[]{:S(2)}, u32[]{:S(2)}) %collective-permute-start) | collective-permute-done | bytes 2359328 | tf_op jit(solution)/shard_map/ppermute | solution.py:17
  134.9 23.1 %collective-permute-done.1 = bf16[2,12,192,256]{3,2,1,0:T(8,128)(2,1)} collective-permute-done((bf16[2,12,192,256]{3,2,1,0:T(8,128)(2,1)S(1)}, bf16[2,12,192,256]{3,2,1,0:T(8,128)(2,1)}, u32[]{:S(2)}, u32[]{:S(2)}) %collective-permute-start.1) | collective-permute-done | bytes 2359328 | tf_op jit(solution)/shard_map/ppermute | solution.py:17
  169.9 6.6 gather_fusion.1
  176.5 5.0 gather_fusion
  187.7 10.1 copy.78
  197.7 6.4 all-to-all-start.1
  204.1 34.1 %copy.68 = bf16[8,2,12,192,256]{3,0,2,1,4:T(8,128)(2,1)} copy(bf16[8,2,12,192,256]{4,3,2,1,0:T(8,128)(2,1)} %param.10) | data formatting | bytes 37748736 | tf_op args[2]
  238.2 101.2 %all-to-all-done.1 = f32[256,2,12,192]{3,1,2,0:T(2,128)} async-done(((f32[256,2,12,192]{3,1,2,0:T(2,128)}), f32[256,2,12,192]{3,1,2,0:T(2,128)}, u32[]{:S(2)}, u32[]{:S(2)}) %all-to-all-start.1) | async-done | bytes 4718624 | tf_op jit(solution)/shard_map/all_to_all | solution.py:91
  339.4 7.9 all-to-all-start
  351.1 4.8 copy.79
  363.0 523.8 %all-to-all-done = bf16[256,8,2,12,192]{4,1,3,2,0:T(8,128)(2,1)} async-done(((bf16[256,8,2,12,192]{4,1,3,2,0:T(8,128)(2,1)}), bf16[256,8,2,12,192]{4,1,3,2,0:T(8,128)(2,1)}, u32[]{:S(2)}, u32[]{:S(2)}) %all-to-all-start) | async-done | bytes 18874400 | tf_op jit(solution)/shard_map/all_to_all | solution.py:77
  886.8 21.2 %copy.69 = bf16[16,8,2,16,12,192]{5,1,4,3,2,0:T(8,128)(2,1)} copy(bf16[16,8,2,16,12,192]{5,1,4,2,0,3:T(8,128)(2,1)} %bitcast.4) | data formatting | bytes 37748736 | tf_op jit(solution)/shard_map/all_to_all | solution.py:77
  908.0 9.8 fusion.77
  917.8 15.8 %fusion.2 = (bf16[16,8,1,192,192]{4,3,2,1,0:T(8,128)(2,1)}, bf16[16,8,1,192,192]{4,3,2,1,0:T(8,128)(2,1)}) fusion(f32[16,192,192]{2,1,0:T(8,128)S(1)} %copy-done.2, f32[16,192,192]{2,1,0:T(8,128)S(1)} %copy.81, bf16[16,8,1,192,192]{4,1,3,2,0:T(8,128)(2,1)S(1)} %get-tuple-element.15, bf16[16,8,1,192,192]{4,1,3,2,0:T(8,128)(2,1)S(1)} %get-tuple-element.14), kind=kLoop, calls=%fused_computation.17 | loop fusion | flops 47185920 | bytes 42467328 | tf_op jit(solution)/shard_map/convert.4
  933.6 22.6 %fusion.16 = bf16[2,192,16,8,192,1]{4,1,5,3,2,0:T(8,128)(2,1)} fusion(bf16[16,8,1,192,192]{4,3,2,1,0:T(8,128)(2,1)} %get-tuple-element.13, bf16[16,8,1,192,192]{4,3,2,1,0:T(8,128)(2,1)} %get-tuple-element.12, bf16[1,192,2,192]{3,1,2,0:T(8,128)(2,1)S(1)} %get-tuple-element.23, bf16[1,192,2,192]{3,1,2,0:T(8,128)(2,1)S(1)} %get-tuple-element.24), kind=kOutput, calls=%fused_computation.30 | convolution fusion | flops 7286095872 | bytes 38043648 | tf_op jit(solution)/shard_map/zcpxj,qkpj->zcqxk/dot_general | solution.py:33
  956.3 22.4 %fusion.15 = bf16[16,8,2,192,192,1]{4,3,1,0,2,5:T(8,128)(2,1)} fusion(f32[192,192]{1,0:T(8,128)S(1)} %copy-done.11, bf16[2,192,16,8,192,1]{4,1,5,3,2,0:T(8,128)(2,1)} %fusion.16, bf16[1,192,2,192]{3,1,2,0:T(8,128)(2,1)S(1)} %get-tuple-element.23, bf16[1,192,2,192]{3,1,2,0:T(8,128)(2,1)S(1)} %get-tuple-element.24), kind=kOutput, calls=%fused_computation.28 | convolution fusion | flops 7267221504 | bytes 38191104 | tf_op jit(solution)/shard_map/zcpjy,qkpj->zcqky/dot_general | solution.py:37
  978.7 34.7 %fusion.21 = f32[16,8,2,192,192]{4,3,2,1,0:T(8,128)} fusion(bf16[16,8,2,192,192,1]{4,3,1,0,2,5:T(8,128)(2,1)} %fusion.15, bf16[1,192,2,192]{3,1,2,0:T(8,128)(2,1)S(1)} %copy-done.9, bf16[1,192,2,192]{3,1,2,0:T(8,128)(2,1)S(1)} %copy-done.8), kind=kOutput, calls=%fused_computation.35 | convolution fusion | flops 14506131456 | bytes 56918016 | tf_op jit(solution)/shard_map/zcpxj,qkpj->zcqxk/dot_general | solution.py:33
  1013.4 26.0 %fusion.6 = (bf16[16,192,192]{2,1,0:T(8,128)(2,1)S(1)}, bf16[16,192,192]{2,1,0:T(8,128)(2,1)S(1)}) fusion(f32[16,8,2,192,192]{4,3,2,1,0:T(8,128)} %fusion.21, bf16[16,8,1,192,192]{4,1,3,2,0:T(8,128)(2,1)} %copy-done.1, bf16[16,8,1,192,192]{4,1,3,2,0:T(8,128)(2,1)} %copy-done), kind=kLoop, calls=%fused_computation.21 | loop fusion | flops 46006272 | bytes 58982400 | tf_op jit(solution)/shard_map/reduce_sum | solution.py:53
  1045.4 3.9 copy.89
  1049.3 7.2 all-to-all-start.2
  1056.6 67.8 %all-to-all-done.2 = bf16[16,2,192,192]{3,0,1,2:T(8,128)(2,1)S(1)} async-done(((bf16[16,2,192,192]{3,0,1,2:T(8,128)(2,1)}), bf16[16,2,192,192]{3,0,1,2:T(8,128)(2,1)S(1)}, u32[]{:S(2)}, u32[]{:S(2)}) %all-to-all-start.2) | async-done | bytes 2359328 | tf_op jit(solution)/shard_map/all_to_all | solution.py:98
  1135.7 10.8 broadcast_in_dim.8
  1146.6 14.6 scatter_fusion
  1161.2 14.7 scatter_fusion.1
  1175.9 7.7 slice_bitcast_fusion.3
  1188.5 3.7 collective-permute-start.6
  1192.2 5.4 collective-permute-start.7
  1197.6 245.1 %collective-permute-done.4 = f32[2,36,64,256]{3,2,1,0:T(8,128)S(1)} collective-permute-done((f32[2,36,64,256]{3,2,1,0:T(8,128)S(1)}, f32[2,36,64,256]{3,2,1,0:T(8,128)S(1)}, u32[]{:S(2)}, u32[]{:S(2)}) %collective-permute-start.4) | collective-permute-done | bytes 4718624 | tf_op jit(solution)/shard_map/ppermute | solution.py:17
  1442.7 50.3 %collective-permute-done.5 = f32[2,36,64,256]{3,2,1,0:T(8,128)S(1)} collective-permute-done((f32[2,36,64,256]{3,2,1,0:T(8,128)S(1)}, f32[2,36,64,256]{3,2,1,0:T(8,128)S(1)}, u32[]{:S(2)}, u32[]{:S(2)}) %collective-permute-start.5) | collective-permute-done | bytes 4718624 | tf_op jit(solution)/shard_map/ppermute | solution.py:17
  1497.3 13.2 fusion.32
  1510.6 7.8 fusion.34
  (74 shorter events, 72.5 us)
Async XLA Ops:
  0.0 17.0 %copy-start.14 = (s32[1,36,2]{1,2,0:T(2,128)S(1)}, s32[1,36,2]{1,2,0:T(2,128)}, u32[]{:S(2)}) copy-start(s32[1,36,2]{1,2,0:T(2,128)} %param.12) | copy-start | bytes 868
  2.7 128.9 %collective-permute-start = (bf16[2,12,192,256]{3,2,1,0:T(8,128)(2,1)S(1)}, bf16[2,12,192,256]{3,2,1,0:T(8,128)(2,1)}, u32[]{:S(2)}, u32[]{:S(2)}) collective-permute-start(bf16[2,12,192,256]{3,2,1,0:T(8,128)(2,1)S(1)} %convert_element_type.99), channel_id=1, source_target_pairs={{0,2},{1,3},{2,4},{3,5},{4,6},{5,7},{6,8},{7,9},{8,10},{9,11},{10,... | collective-permute-start | bytes 7077896 | tf_op jit(solution)/shard_map/ppermute | solution.py:17
  5.8 152.2 %collective-permute-start.1 = (bf16[2,12,192,256]{3,2,1,0:T(8,128)(2,1)S(1)}, bf16[2,12,192,256]{3,2,1,0:T(8,128)(2,1)}, u32[]{:S(2)}, u32[]{:S(2)}) collective-permute-start(bf16[2,12,192,256]{3,2,1,0:T(8,128)(2,1)S(1)} %convert_element_type.99), channel_id=1, source_target_pairs={{0,1},{1,2},{2,3},{3,4},{4,5},{5,6},{6,7},{7,8},{8,9},{9,10},{10,1... | collective-permute-start | bytes 7077896 | tf_op jit(solution)/shard_map/ppermute | solution.py:17
  9.8 153.4 %collective-permute-start.2 = (bf16[2,12,192,256]{3,2,1,0:T(8,128)(2,1)S(1)}, bf16[2,12,192,256]{3,2,1,0:T(8,128)(2,1)}, u32[]{:S(2)}, u32[]{:S(2)}) collective-permute-start(bf16[2,12,192,256]{3,2,1,0:T(8,128)(2,1)S(1)} %convert_element_type.99), channel_id=1, source_target_pairs={{1,0},{2,1},{3,2},{4,3},{5,4},{6,5},{7,6},{8,7},{9,8},{10,9},{11,1... | collective-permute-start | bytes 7077896 | tf_op jit(solution)/shard_map/ppermute | solution.py:17
  11.8 154.8 %collective-permute-start.3 = (bf16[2,12,192,256]{3,2,1,0:T(8,128)(2,1)S(1)}, bf16[2,12,192,256]{3,2,1,0:T(8,128)(2,1)}, u32[]{:S(2)}, u32[]{:S(2)}) collective-permute-start(bf16[2,12,192,256]{3,2,1,0:T(8,128)(2,1)S(1)} %convert_element_type.99), channel_id=1, source_target_pairs={{2,0},{3,1},{4,2},{5,3},{6,4},{7,5},{8,6},{9,7},{10,8},{11,9},{12,... | collective-permute-start | bytes 7077896 | tf_op jit(solution)/shard_map/ppermute | solution.py:17
  17.0 167.0 %copy-start.3 = (bf16[36,2,64,64]{3,2,1,0:T(8,128)(2,1)}, bf16[36,2,64,64]{3,2,1,0:T(8,128)(2,1)S(1)}, u32[]{:S(2)}) copy-start(bf16[36,2,64,64]{3,2,1,0:T(8,128)(2,1)S(1)} %reshape_squeeze.3) | copy-start | bytes 1769476
  17.0 0.7 copy-start.12
  17.7 143.6 %slice-start = ((s8[4718592]{0:T(1024)(128)(4,1)}), s8[4194304]{0:T(1024)(128)(4,1)S(1)}, s32[]{:S(2)}) async-start(s8[4718592]{0:T(1024)(128)(4,1)} %bitcast.213), calls=%async_computation.3 | async-start | bytes 8388608
  17.7 143.6 %slice-start.1 = ((s8[4718592]{0:T(1024)(128)(4,1)}), s8[524288]{0:T(1024)(128)(4,1)S(1)}, s32[]{:S(2)}) async-start(s8[4718592]{0:T(1024)(128)(4,1)} %bitcast.213), calls=%async_computation.4 | async-start | bytes 1048576
  197.7 141.6 %all-to-all-start.1 = ((f32[256,2,12,192]{3,1,2,0:T(2,128)}), f32[256,2,12,192]{3,1,2,0:T(2,128)}, u32[]{:S(2)}, u32[]{:S(2)}) async-start(f32[256,2,12,192]{3,1,2,0:T(2,128)} %copy.78), calls=%async_computation.1 | async-start | bytes 12582912 | tf_op jit(solution)/shard_map/all_to_all | solution.py:91
  339.4 11.1 copy-start.10
  339.4 547.4 %all-to-all-start = ((bf16[256,8,2,12,192]{4,1,3,2,0:T(8,128)(2,1)}), bf16[256,8,2,12,192]{4,1,3,2,0:T(8,128)(2,1)}, u32[]{:S(2)}, u32[]{:S(2)}) async-start(bf16[256,8,2,12,192]{4,1,3,2,0:T(8,128)(2,1)} %bitcast.212), calls=%async_computation | async-start | bytes 50331648 | tf_op jit(solution)/shard_map/all_to_all | solution.py:77
  908.0 9.8 copy-start.2
  917.8 15.9 %copy-start = (bf16[16,8,1,192,192]{4,1,3,2,0:T(8,128)(2,1)}, bf16[16,8,1,192,192]{4,1,3,2,0:T(8,128)(2,1)S(1)}, u32[]{:S(2)}) copy-start(bf16[16,8,1,192,192]{4,1,3,2,0:T(8,128)(2,1)S(1)} %get-tuple-element.14) | copy-start | bytes 28311556
  917.8 15.8 %copy-start.1 = (bf16[16,8,1,192,192]{4,1,3,2,0:T(8,128)(2,1)}, bf16[16,8,1,192,192]{4,1,3,2,0:T(8,128)(2,1)S(1)}, u32[]{:S(2)}) copy-start(bf16[16,8,1,192,192]{4,1,3,2,0:T(8,128)(2,1)S(1)} %get-tuple-element.15) | copy-start | bytes 28311556
  933.6 22.6 %copy-start.11 = (f32[192,192]{1,0:T(8,128)S(1)}, f32[192,192]{1,0:T(8,128)}, u32[]{:S(2)}) copy-start(f32[192,192]{1,0:T(8,128)} %convert_bitcast_fusion.2) | copy-start | bytes 442372
  956.3 22.4 %copy-start.8 = (bf16[1,192,2,192]{3,1,2,0:T(8,128)(2,1)S(1)}, bf16[1,192,2,192]{3,1,2,0:T(8,128)(2,1)}, u32[]{:S(2)}) copy-start(bf16[1,192,2,192]{3,1,2,0:T(8,128)(2,1)} %get-tuple-element.22) | copy-start | bytes 442372
  956.3 22.4 %copy-start.9 = (bf16[1,192,2,192]{3,1,2,0:T(8,128)(2,1)S(1)}, bf16[1,192,2,192]{3,1,2,0:T(8,128)(2,1)}, u32[]{:S(2)}) copy-start(bf16[1,192,2,192]{3,1,2,0:T(8,128)(2,1)} %get-tuple-element.25) | copy-start | bytes 442372
  1049.3 7.2 copy-start.13
  1049.3 75.0 %all-to-all-start.2 = ((bf16[16,2,192,192]{3,0,1,2:T(8,128)(2,1)}), bf16[16,2,192,192]{3,0,1,2:T(8,128)(2,1)S(1)}, u32[]{:S(2)}, u32[]{:S(2)}) async-start(bf16[16,2,192,192]{3,0,1,2:T(8,128)(2,1)} %copy.89), calls=%async_computation.2 | async-start | bytes 6291456 | tf_op jit(solution)/shard_map/all_to_all | solution.py:98
  1126.4 3.3 copy-start.4
  1183.6 259.1 %collective-permute-start.4 = (f32[2,36,64,256]{3,2,1,0:T(8,128)S(1)}, f32[2,36,64,256]{3,2,1,0:T(8,128)S(1)}, u32[]{:S(2)}, u32[]{:S(2)}) collective-permute-start(f32[2,36,64,256]{3,2,1,0:T(8,128)S(1)} %get-tuple-element.17), channel_id=1, source_target_pairs={{2,0},{3,1},{4,2},{5,3},{6,4},{7,5},{8,6},{9,7},{10,8},{11,9},{12,... | collective-permute-start | bytes 14155784 | tf_op jit(solution)/shard_map/ppermute | solution.py:17
  1185.5 307.4 %collective-permute-start.5 = (f32[2,36,64,256]{3,2,1,0:T(8,128)S(1)}, f32[2,36,64,256]{3,2,1,0:T(8,128)S(1)}, u32[]{:S(2)}, u32[]{:S(2)}) collective-permute-start(f32[2,36,64,256]{3,2,1,0:T(8,128)S(1)} %get-tuple-element.16), channel_id=1, source_target_pairs={{1,0},{2,1},{3,2},{4,3},{5,4},{6,5},{7,6},{8,7},{9,8},{10,9},{11,1... | collective-permute-start | bytes 14155784 | tf_op jit(solution)/shard_map/ppermute | solution.py:17
  1188.5 304.5 %collective-permute-start.6 = (f32[2,36,64,256]{3,2,1,0:T(8,128)S(1)}, f32[2,36,64,256]{3,2,1,0:T(8,128)S(1)}, u32[]{:S(2)}, u32[]{:S(2)}) collective-permute-start(f32[2,36,64,256]{3,2,1,0:T(8,128)S(1)} %get-tuple-element.19), channel_id=1, source_target_pairs={{0,1},{1,2},{2,3},{3,4},{4,5},{5,6},{6,7},{7,8},{8,9},{9,10},{10,1... | collective-permute-start | bytes 14155784 | tf_op jit(solution)/shard_map/ppermute | solution.py:17
  1192.2 305.1 %collective-permute-start.7 = (f32[2,36,64,256]{3,2,1,0:T(8,128)S(1)}, f32[2,36,64,256]{3,2,1,0:T(8,128)}, u32[]{:S(2)}, u32[]{:S(2)}) collective-permute-start(f32[2,36,64,256]{3,2,1,0:T(8,128)S(1)} %get-tuple-element.18), channel_id=1, source_target_pairs={{0,2},{1,3},{2,4},{3,5},{4,6},{5,7},{6,8},{7,9},{8,10},{9,11},{10,... | collective-permute-start | bytes 14155784 | tf_op jit(solution)/shard_map/ppermute | solution.py:17
  1442.7 50.3 %copy-start.5 = (f32[2,36,64,256]{3,2,1,0:T(8,128)}, f32[2,36,64,256]{3,2,1,0:T(8,128)S(1)}, u32[]{:S(2)}) copy-start(f32[2,36,64,256]{3,2,1,0:T(8,128)S(1)} %collective-permute-done.4) | copy-start | bytes 14155780
  1492.9 2.2 copy-start.6
  1495.1 2.2 copy-start.7
where the time goes:
time: 1530 us; the launch traced here: 1520 us
  waiting for transfers between devices  1130 us (74%)
  local copies, waits for them, and re-layouts  153 us (10%)
  other arithmetic  103 us (7%)
  matrix products  89.1 us (6%)
  starting transfers between devices  47.5 us (3%)
    all_to_all x1, waiting for transfers between devices, per_device(): lax.all_to_all(maps_leading, 'slab', split_axis=0, concat_axis=3, tiled=T...  524 us
    ppermute x8, waiting for transfers between devices, shifted(): return lax.ppermute(shard, axis, pairs)  432 us
    all_to_all x1, waiting for transfers between devices, per_device(): lax.all_to_all(warped_leading, 'slab', split_axis=0, concat_axis=2, tiled...  101 us
    all_to_all x1, waiting for transfers between devices, per_device(): lax.all_to_all(combined_columns, 'slab', split_axis=2, concat_axis=0, til...  67.8 us
    dot_general x2, matrix products, column_y(): jnp.einsum('zcpxj,qkpj->zcqxk', volume, matrix, preferred_element_type=jn...  57.3 us
    unnamed x40, local copies, waits for them, and re-layouts  52.6 us
  transfers between devices with their start and end apart: 11, of which 7 were waited for; matrix products, arithmetic and copies ran while one was open for 4% of the time, Pallas kernels for 0%

commit v1 on v0

--- a/solution.py
+++ b/solution.py
@@ -88,7 +88,17 @@
     warped = warped.reshape(2, planes, NY, NZ)
     sampled = masks[0].astype(jnp.float32)
     warped_leading = jnp.transpose(warped, (3, 0, 1, 2))
-    warped_columns = lax.all_to_all(warped_leading, "slab", split_axis=0, concat_axis=2, tiled=True)
+
+    def side_time(view, on_dim, along_dim):
+        current_value = lax.all_to_all(
+            jnp.stack(jnp.split(view, lax.axis_size("slab"), axis=on_dim), axis=0),
+            concat_axis=0,
+            axis_name="slab",
+            split_axis=0,
+        )
+        return jnp.concatenate(current_value, along_dim)
+
+    warped_columns = side_time(warped_leading, 0, 2)
     spectra = column_y(expand_columns(maps_columns, warped_columns), forward_y).astype(jnp.bfloat16)
     middle = (column_x(spectra, forward_x) * sampled[None, None, None, :, :]).astype(jnp.bfloat16)
     restored = column_x(middle, inverse_x).astype(jnp.bfloat16)

time: 1530 us -> 1590 us (1.039)
  local copies, waits for them, and re-layouts: 153 us -> 216 us
    another operation x0 -> x18, local copies, waits for them, and re-layouts: none -> 59.3 us  [side_time(): jnp.stack(jnp.split(view, lax.axis_size('slab'), axis=on_dim), axis=0)]
    unnamed x40 -> x75, local copies, waits for them, and re-layouts: 52.6 us -> 70.6 us
where the time goes in v1:
time: 1590 us; the launch traced here: 1580 us
  waiting for transfers between devices  1130 us (71%)
  local copies, waits for them, and re-layouts  216 us (14%)
  other arithmetic  102 us (6%)
  matrix products  89.5 us (6%)
  starting transfers between devices  47.7 us (3%)
    all_to_all x1, waiting for transfers between devices, per_device(): lax.all_to_all(maps_leading, 'slab', split_axis=0, concat_axis=3, tiled=T...  526 us
    ppermute x8, waiting for transfers between devices, shifted(): return lax.ppermute(shard, axis, pairs)  432 us
    all_to_all x1, waiting for transfers between devices, side_time(): lax.all_to_all(jnp.stack(jnp.split(view, lax.axis_size('slab'), axis=on_d...  101 us
    unnamed x75, local copies, waits for them, and re-layouts  70.6 us
    all_to_all x1, waiting for transfers between devices, per_device(): lax.all_to_all(combined_columns, 'slab', split_axis=2, concat_axis=0, til...  67.8 us
    another operation x18, local copies, waits for them, and re-layouts, side_time(): jnp.stack(jnp.split(view, lax.axis_size('slab'), axis=on_dim), axis=0)  59.3 us
    dot_general x2, matrix products, column_y(): jnp.einsum('zcpxj,qkpj->zcqxk', volume, matrix, preferred_element_type=jn...  57.8 us
  transfers between devices with their start and end apart: 11, of which 7 were waited for; matrix products, arithmetic and copies ran while one was open for 4% of the time, Pallas kernels for 0%

profile of v1, /device:TPU:9, one launch (start us, length us, event | category | flops | bytes accessed | tf_op | source)
XLA Modules:
  0.0 1583.5 jit_solution(6379233890252979142)
XLA Ops:
  5.8 4.0 collective-permute-start.1
  17.7 113.9 %collective-permute-done = bf16[2,12,192,256]{3,2,1,0:T(8,128)(2,1)} collective-permute-done((bf16[2,12,192,256]{3,2,1,0:T(8,128)(2,1)S(1)}, bf16[2,12,192,256]{3,2,1,0:T(8,128)(2,1)}, u32[]{:S(2)}, u32[]{:S(2)}) %collective-permute-start) | collective-permute-done | bytes 2359328 | tf_op jit(solution)/shard_map/ppermute | solution.py:17
  134.9 23.1 %collective-permute-done.1 = bf16[2,12,192,256]{3,2,1,0:T(8,128)(2,1)} collective-permute-done((bf16[2,12,192,256]{3,2,1,0:T(8,128)(2,1)S(1)}, bf16[2,12,192,256]{3,2,1,0:T(8,128)(2,1)}, u32[]{:S(2)}, u32[]{:S(2)}) %collective-permute-start.1) | collective-permute-done | bytes 2359328 | tf_op jit(solution)/shard_map/ppermute | solution.py:17
  169.8 6.6 gather_fusion.1
  176.5 5.0 gather_fusion
  185.4 15.4 slice_bitcast_fusion.7
  262.7 6.4 all-to-all-start.1
  269.1 34.1 %copy.49 = bf16[8,2,12,192,256]{3,0,2,1,4:T(8,128)(2,1)} copy(bf16[8,2,12,192,256]{4,3,2,1,0:T(8,128)(2,1)} %param.10) | data formatting | bytes 37748736 | tf_op args[2]
  303.1 101.2 %all-to-all-done.1 = f32[16,16,2,12,192]{4,1,3,2,0:T(8,128)} async-done(((f32[16,16,2,12,192]{4,1,3,2,0:T(8,128)}), f32[16,16,2,12,192]{4,1,3,2,0:T(8,128)}, u32[]{:S(2)}, u32[]{:S(2)}) %all-to-all-start.1) | async-done | bytes 4718624 | tf_op jit(solution)/shard_map/all_to_all | solution.py:93
  404.3 7.5 all-to-all-start
  415.8 3.5 copy.75
  425.4 526.1 %all-to-all-done = bf16[256,8,2,12,192]{4,1,3,2,0:T(8,128)(2,1)} async-done(((bf16[256,8,2,12,192]{4,1,3,2,0:T(8,128)(2,1)}), bf16[256,8,2,12,192]{4,1,3,2,0:T(8,128)(2,1)}, u32[]{:S(2)}, u32[]{:S(2)}) %all-to-all-start) | async-done | bytes 18874400 | tf_op jit(solution)/shard_map/all_to_all | solution.py:77
  951.4 21.1 %copy.50 = bf16[16,8,2,16,12,192]{5,1,4,3,2,0:T(8,128)(2,1)} copy(bf16[16,8,2,16,12,192]{5,1,4,2,0,3:T(8,128)(2,1)} %bitcast.4) | data formatting | bytes 37748736 | tf_op jit(solution)/shard_map/all_to_all | solution.py:77
  972.6 9.8 fusion.77
  982.4 15.9 %fusion.2 = (bf16[16,8,1,192,192]{4,3,2,1,0:T(8,128)(2,1)}, bf16[16,8,1,192,192]{4,3,2,1,0:T(8,128)(2,1)}) fusion(f32[16,192,192]{2,1,0:T(8,128)S(1)} %copy-done.2, f32[16,192,192]{2,1,0:T(8,128)S(1)} %copy.76, bf16[16,8,1,192,192]{4,1,3,2,0:T(8,128)(2,1)S(1)} %get-tuple-element.15, bf16[16,8,1,192,192]{4,1,3,2,0:T(8,128)(2,1)S(1)} %get-tuple-element.14), kind=kLoop, calls=%fused_computation.17 | loop fusion | flops 47185920 | bytes 42467328 | tf_op jit(solution)/shard_map/convert.4
  998.3 23.0 %fusion.16 = bf16[2,192,16,8,192,1]{4,1,5,3,2,0:T(8,128)(2,1)} fusion(bf16[16,8,1,192,192]{4,3,2,1,0:T(8,128)(2,1)} %get-tuple-element.13, bf16[16,8,1,192,192]{4,3,2,1,0:T(8,128)(2,1)} %get-tuple-element.12, bf16[1,192,2,192]{3,1,2,0:T(8,128)(2,1)S(1)} %get-tuple-element.39, bf16[1,192,2,192]{3,1,2,0:T(8,128)(2,1)S(1)} %get-tuple-element.40), kind=kOutput, calls=%fused_computation.30 | convolution fusion | flops 7286095872 | bytes 38043648 | tf_op jit(solution)/shard_map/zcpxj,qkpj->zcqxk/dot_general | solution.py:33
  1021.3 22.4 %fusion.15 = bf16[16,8,2,192,192,1]{4,3,1,0,2,5:T(8,128)(2,1)} fusion(f32[192,192]{1,0:T(8,128)S(1)} %copy-done.21, bf16[2,192,16,8,192,1]{4,1,5,3,2,0:T(8,128)(2,1)} %fusion.16, bf16[1,192,2,192]{3,1,2,0:T(8,128)(2,1)S(1)} %get-tuple-element.39, bf16[1,192,2,192]{3,1,2,0:T(8,128)(2,1)S(1)} %get-tuple-element.40), kind=kOutput, calls=%fused_computation.28 | convolution fusion | flops 7267221504 | bytes 38191104 | tf_op jit(solution)/shard_map/zcpjy,qkpj->zcqky/dot_general | solution.py:37
  1043.8 34.7 %fusion.21 = f32[16,8,2,192,192]{4,3,2,1,0:T(8,128)} fusion(bf16[16,8,2,192,192,1]{4,3,1,0,2,5:T(8,128)(2,1)} %fusion.15, bf16[1,192,2,192]{3,1,2,0:T(8,128)(2,1)S(1)} %copy-done.19, bf16[1,192,2,192]{3,1,2,0:T(8,128)(2,1)S(1)} %copy-done.18), kind=kOutput, calls=%fused_computation.35 | convolution fusion | flops 14506131456 | bytes 56918016 | tf_op jit(solution)/shard_map/zcpxj,qkpj->zcqxk/dot_general | solution.py:33
  1078.5 25.8 %fusion.6 = (bf16[16,192,192]{2,1,0:T(8,128)(2,1)S(1)}, bf16[16,192,192]{2,1,0:T(8,128)(2,1)S(1)}) fusion(f32[16,8,2,192,192]{4,3,2,1,0:T(8,128)} %fusion.21, bf16[16,8,1,192,192]{4,1,3,2,0:T(8,128)(2,1)} %copy-done.1, bf16[16,8,1,192,192]{4,1,3,2,0:T(8,128)(2,1)} %copy-done), kind=kLoop, calls=%fused_computation.21 | loop fusion | flops 46006272 | bytes 58982400 | tf_op jit(solution)/shard_map/reduce_sum | solution.py:53
  1110.4 3.9 copy.84
  1114.3 7.2 all-to-all-start.2
  1121.5 67.8 %all-to-all-done.2 = bf16[16,2,192,192]{3,0,1,2:T(8,128)(2,1)S(1)} async-done(((bf16[16,2,192,192]{3,0,1,2:T(8,128)(2,1)}), bf16[16,2,192,192]{3,0,1,2:T(8,128)(2,1)S(1)}, u32[]{:S(2)}, u32[]{:S(2)}) %all-to-all-start.2) | async-done | bytes 2359328 | tf_op jit(solution)/shard_map/all_to_all | solution.py:108
  1200.7 10.8 broadcast_in_dim.8
  1211.5 14.3 scatter_fusion
  1225.8 14.3 scatter_fusion.1
  1240.1 7.7 slice_bitcast_fusion.3
  1252.4 4.7 collective-permute-start.6
  1257.1 5.2 collective-permute-start.7
  1262.4 245.1 %collective-permute-done.4 = f32[2,36,64,256]{3,2,1,0:T(8,128)S(1)} collective-permute-done((f32[2,36,64,256]{3,2,1,0:T(8,128)S(1)}, f32[2,36,64,256]{3,2,1,0:T(8,128)S(1)}, u32[]{:S(2)}, u32[]{:S(2)}) %collective-permute-start.4) | collective-permute-done | bytes 4718624 | tf_op jit(solution)/shard_map/ppermute | solution.py:17
  1507.5 50.4 %collective-permute-done.5 = f32[2,36,64,256]{3,2,1,0:T(8,128)S(1)} collective-permute-done((f32[2,36,64,256]{3,2,1,0:T(8,128)S(1)}, f32[2,36,64,256]{3,2,1,0:T(8,128)S(1)}, u32[]{:S(2)}, u32[]{:S(2)}) %collective-permute-start.5) | collective-permute-done | bytes 4718624 | tf_op jit(solution)/shard_map/ppermute | solution.py:17
  1562.2 13.2 fusion.32
  1575.5 7.8 fusion.34
  (125 shorter events, 130.8 us)
Async XLA Ops:
  0.0 17.0 %copy-start.24 = (s32[1,36,2]{1,2,0:T(2,128)S(1)}, s32[1,36,2]{1,2,0:T(2,128)}, u32[]{:S(2)}) copy-start(s32[1,36,2]{1,2,0:T(2,128)} %param.12) | copy-start | bytes 868
  2.7 128.9 %collective-permute-start = (bf16[2,12,192,256]{3,2,1,0:T(8,128)(2,1)S(1)}, bf16[2,12,192,256]{3,2,1,0:T(8,128)(2,1)}, u32[]{:S(2)}, u32[]{:S(2)}) collective-permute-start(bf16[2,12,192,256]{3,2,1,0:T(8,128)(2,1)S(1)} %convert_element_type.99), channel_id=1, source_target_pairs={{0,2},{1,3},{2,4},{3,5},{4,6},{5,7},{6,8},{7,9},{8,10},{9,11},{10,... | collective-permute-start | bytes 7077896 | tf_op jit(solution)/shard_map/ppermute | solution.py:17
  5.8 152.2 %collective-permute-start.1 = (bf16[2,12,192,256]{3,2,1,0:T(8,128)(2,1)S(1)}, bf16[2,12,192,256]{3,2,1,0:T(8,128)(2,1)}, u32[]{:S(2)}, u32[]{:S(2)}) collective-permute-start(bf16[2,12,192,256]{3,2,1,0:T(8,128)(2,1)S(1)} %convert_element_type.99), channel_id=1, source_target_pairs={{0,1},{1,2},{2,3},{3,4},{4,5},{5,6},{6,7},{7,8},{8,9},{9,10},{10,1... | collective-permute-start | bytes 7077896 | tf_op jit(solution)/shard_map/ppermute | solution.py:17
  9.8 153.4 %collective-permute-start.2 = (bf16[2,12,192,256]{3,2,1,0:T(8,128)(2,1)S(1)}, bf16[2,12,192,256]{3,2,1,0:T(8,128)(2,1)}, u32[]{:S(2)}, u32[]{:S(2)}) collective-permute-start(bf16[2,12,192,256]{3,2,1,0:T(8,128)(2,1)S(1)} %convert_element_type.99), channel_id=1, source_target_pairs={{1,0},{2,1},{3,2},{4,3},{5,4},{6,5},{7,6},{8,7},{9,8},{10,9},{11,1... | collective-permute-start | bytes 7077896 | tf_op jit(solution)/shard_map/ppermute | solution.py:17
  11.8 154.8 %collective-permute-start.3 = (bf16[2,12,192,256]{3,2,1,0:T(8,128)(2,1)S(1)}, bf16[2,12,192,256]{3,2,1,0:T(8,128)(2,1)}, u32[]{:S(2)}, u32[]{:S(2)}) collective-permute-start(bf16[2,12,192,256]{3,2,1,0:T(8,128)(2,1)S(1)} %convert_element_type.99), channel_id=1, source_target_pairs={{2,0},{3,1},{4,2},{5,3},{6,4},{7,5},{8,6},{9,7},{10,8},{11,9},{12,... | collective-permute-start | bytes 7077896 | tf_op jit(solution)/shard_map/ppermute | solution.py:17
  17.0 167.0 %copy-start.3 = (bf16[36,2,64,64]{3,2,1,0:T(8,128)(2,1)}, bf16[36,2,64,64]{3,2,1,0:T(8,128)(2,1)S(1)}, u32[]{:S(2)}) copy-start(bf16[36,2,64,64]{3,2,1,0:T(8,128)(2,1)S(1)} %reshape_squeeze.3) | copy-start | bytes 1769476
  17.7 143.7 %slice-start = ((s8[4718592]{0:T(1024)(128)(4,1)}), s8[4194304]{0:T(1024)(128)(4,1)S(1)}, s32[]{:S(2)}) async-start(s8[4718592]{0:T(1024)(128)(4,1)} %bitcast.245), calls=%async_computation.3 | async-start | bytes 8388608
  17.7 143.7 %slice-start.1 = ((s8[4718592]{0:T(1024)(128)(4,1)}), s8[524288]{0:T(1024)(128)(4,1)S(1)}, s32[]{:S(2)}) async-start(s8[4718592]{0:T(1024)(128)(4,1)} %bitcast.245), calls=%async_computation.4 | async-start | bytes 1048576
  200.8 10.0 copy-start.8
  212.4 9.9 copy-start.7
  223.9 10.0 copy-start.6
  244.8 10.8 copy-start.17
  244.8 11.7 copy-start.16
  244.8 12.4 copy-start.15
  244.8 13.2 copy-start.14
  244.8 14.0 copy-start.13
  244.8 14.7 copy-start.12
  262.7 141.6 %all-to-all-start.1 = ((f32[16,16,2,12,192]{4,1,3,2,0:T(8,128)}), f32[16,16,2,12,192]{4,1,3,2,0:T(8,128)}, u32[]{:S(2)}, u32[]{:S(2)}) async-start(f32[16,16,2,12,192]{4,1,3,2,0:T(8,128)} %constant_dynamic-update-slice_fusion), calls=%async_computation.1 | async-start | bytes 12582912 | tf_op jit(solution)/shard_map/all_to_all | solution.py:93
  404.3 10.8 copy-start.20
  404.3 547.1 %all-to-all-start = ((bf16[256,8,2,12,192]{4,1,3,2,0:T(8,128)(2,1)}), bf16[256,8,2,12,192]{4,1,3,2,0:T(8,128)(2,1)}, u32[]{:S(2)}, u32[]{:S(2)}) async-start(bf16[256,8,2,12,192]{4,1,3,2,0:T(8,128)(2,1)} %bitcast.244), calls=%async_computation | async-start | bytes 50331648 | tf_op jit(solution)/shard_map/all_to_all | solution.py:77
  972.6 9.8 copy-start.2
  982.4 15.9 %copy-start = (bf16[16,8,1,192,192]{4,1,3,2,0:T(8,128)(2,1)}, bf16[16,8,1,192,192]{4,1,3,2,0:T(8,128)(2,1)S(1)}, u32[]{:S(2)}) copy-start(bf16[16,8,1,192,192]{4,1,3,2,0:T(8,128)(2,1)S(1)} %get-tuple-element.14) | copy-start | bytes 28311556
  982.4 15.9 %copy-start.1 = (bf16[16,8,1,192,192]{4,1,3,2,0:T(8,128)(2,1)}, bf16[16,8,1,192,192]{4,1,3,2,0:T(8,128)(2,1)S(1)}, u32[]{:S(2)}) copy-start(bf16[16,8,1,192,192]{4,1,3,2,0:T(8,128)(2,1)S(1)} %get-tuple-element.15) | copy-start | bytes 28311556
  998.3 23.0 %copy-start.21 = (f32[192,192]{1,0:T(8,128)S(1)}, f32[192,192]{1,0:T(8,128)}, u32[]{:S(2)}) copy-start(f32[192,192]{1,0:T(8,128)} %convert_bitcast_fusion.2) | copy-start | bytes 442372
  1021.3 22.4 %copy-start.18 = (bf16[1,192,2,192]{3,1,2,0:T(8,128)(2,1)S(1)}, bf16[1,192,2,192]{3,1,2,0:T(8,128)(2,1)}, u32[]{:S(2)}) copy-start(bf16[1,192,2,192]{3,1,2,0:T(8,128)(2,1)} %get-tuple-element.38) | copy-start | bytes 442372
  1021.3 22.4 %copy-start.19 = (bf16[1,192,2,192]{3,1,2,0:T(8,128)(2,1)S(1)}, bf16[1,192,2,192]{3,1,2,0:T(8,128)(2,1)}, u32[]{:S(2)}) copy-start(bf16[1,192,2,192]{3,1,2,0:T(8,128)(2,1)} %get-tuple-element.41) | copy-start | bytes 442372
  1114.3 75.0 %all-to-all-start.2 = ((bf16[16,2,192,192]{3,0,1,2:T(8,128)(2,1)}), bf16[16,2,192,192]{3,0,1,2:T(8,128)(2,1)S(1)}, u32[]{:S(2)}, u32[]{:S(2)}) async-start(bf16[16,2,192,192]{3,0,1,2:T(8,128)(2,1)} %copy.84), calls=%async_computation.2 | async-start | bytes 6291456 | tf_op jit(solution)/shard_map/all_to_all | solution.py:108
  1247.8 259.7 %collective-permute-start.4 = (f32[2,36,64,256]{3,2,1,0:T(8,128)S(1)}, f32[2,36,64,256]{3,2,1,0:T(8,128)S(1)}, u32[]{:S(2)}, u32[]{:S(2)}) collective-permute-start(f32[2,36,64,256]{3,2,1,0:T(8,128)S(1)} %get-tuple-element.17), channel_id=1, source_target_pairs={{2,0},{3,1},{4,2},{5,3},{6,4},{7,5},{8,6},{9,7},{10,8},{11,9},{12,... | collective-permute-start | bytes 14155784 | tf_op jit(solution)/shard_map/ppermute | solution.py:17
  1249.7 308.1 %collective-permute-start.5 = (f32[2,36,64,256]{3,2,1,0:T(8,128)S(1)}, f32[2,36,64,256]{3,2,1,0:T(8,128)S(1)}, u32[]{:S(2)}, u32[]{:S(2)}) collective-permute-start(f32[2,36,64,256]{3,2,1,0:T(8,128)S(1)} %get-tuple-element.16), channel_id=1, source_target_pairs={{1,0},{2,1},{3,2},{4,3},{5,4},{6,5},{7,6},{8,7},{9,8},{10,9},{11,1... | collective-permute-start | bytes 14155784 | tf_op jit(solution)/shard_map/ppermute | solution.py:17
  1252.4 305.4 %collective-permute-start.6 = (f32[2,36,64,256]{3,2,1,0:T(8,128)S(1)}, f32[2,36,64,256]{3,2,1,0:T(8,128)S(1)}, u32[]{:S(2)}, u32[]{:S(2)}) collective-permute-start(f32[2,36,64,256]{3,2,1,0:T(8,128)S(1)} %get-tuple-element.19), channel_id=1, source_target_pairs={{0,1},{1,2},{2,3},{3,4},{4,5},{5,6},{6,7},{7,8},{8,9},{9,10},{10,1... | collective-permute-start | bytes 14155784 | tf_op jit(solution)/shard_map/ppermute | solution.py:17
  1257.1 305.1 %collective-permute-start.7 = (f32[2,36,64,256]{3,2,1,0:T(8,128)S(1)}, f32[2,36,64,256]{3,2,1,0:T(8,128)}, u32[]{:S(2)}, u32[]{:S(2)}) collective-permute-start(f32[2,36,64,256]{3,2,1,0:T(8,128)S(1)} %get-tuple-element.18), channel_id=1, source_target_pairs={{0,2},{1,3},{2,4},{3,5},{4,6},{5,7},{6,8},{7,9},{8,10},{9,11},{10,... | collective-permute-start | bytes 14155784 | tf_op jit(solution)/shard_map/ppermute | solution.py:17
  1507.5 50.4 %copy-start.9 = (f32[2,36,64,256]{3,2,1,0:T(8,128)}, f32[2,36,64,256]{3,2,1,0:T(8,128)S(1)}, u32[]{:S(2)}) copy-start(f32[2,36,64,256]{3,2,1,0:T(8,128)S(1)} %collective-permute-done.4) | copy-start | bytes 14155780
  (6 other events, 23.9 us)
